TPU v7x, 32 devices: a whole 2x2x4 slice. The times are simulated.
32 devices in a mesh: groups: 2 (over x), views: 16 (over z, y, core).
Axes of the slice: x: 2, y: 2, z: 4, core: 2. Of those that a mesh axis runs over, the one named last changes fastest.
Arguments:
- tokens: bfloat16 [32, 128, 1024], P(('groups', 'views')), parts along dimension 0, may hold values from -6 to 6
- in_gain: float32 [1024], replicated, may hold values from 0.7 to 6, as said below
- w_query: bfloat16 [1024, 1024], replicated, may hold values from -0.1875 to 0.1875
- w_key: bfloat16 [1024, 1024], replicated, may hold values from -0.1875 to 0.1875
- w_value: bfloat16 [1024, 1024], replicated, may hold values from -0.1875 to 0.1875
- w_out: bfloat16 [1024, 1024], replicated, may hold values from -0.1875 to 0.1875
- out_gain: float32 [1024], replicated, may hold values from 0.1 to 1.9
- covis_list: int32 [32, 12], P(('groups', 'views')), parts along dimension 0, may hold values from 0 to 15, as said below
- covis_count: int32 [32], P(('groups', 'views')), parts along dimension 0, may hold values from 2 to 12
Outputs:
- mixed: bfloat16 [32, 128, 1024], P(('groups', 'views')), parts along dimension 0
There are 2 independent parts, one for each index of `groups`. A program takes and returns all parts, laid end to end along the dimension named above; an argument that names none is the same for every part. Nothing has to cross between parts.
Inputs may be any that keep to these rules, and one draw needn't show every extreme that they name: `covis_list`: row v lists 12 distinct view ids w, each with w - v modulo 16 among -6 to -1 and 1 to 6; only the first covis_count[v] entries are covisible views, the others are not used. `in_gain`: positive gains.
All inputs are finite; a program needn't handle non-finite values.
Results may differ from a plain program's by a relative error of at most 0.0085.
The roundings to bfloat16 on the way count: a program that leaves them out, or rounds other values in their place, can miss the bound.
Values may be sent and summed in bfloat16 or wider, within the bound.
A program may use at most 128 MiB of HBM per device.

v0:
```python
import functools

import jax
import jax.numpy as jnp
from jax import lax
from jax.experimental import pallas as pl
from jax.experimental.pallas import tpu as pltpu
from jax.sharding import PartitionSpec as P

HEADS = 16
HEAD_DIM = 64
REACH = 6
SPAN = REACH // 2
CHUNKS = 2 * SPAN + 1
PARTS = 4
MESH = pl.DeviceIdType.MESH
INF = float("inf")


def is_grid(chips):
    return chips == 2 * SPAN + 2


def ring_position(chip, chips):
    if not is_grid(chips):
        return chip
    row, col = chip // 2, chip % 2
    return row + col * (chips - 1 - 2 * row)


def ring_chip(position, chips):
    position = (position + chips) % chips
    if not is_grid(chips):
        return position
    col = position // (chips // 2)
    row = position + col * (chips - 1 - 2 * position)
    return 2 * row + col


def ring_route(chips):
    route = {1: (0, -1), 2: (0, 1)}
    last = CHUNKS + 1 if is_grid(chips) else CHUNKS
    for slot in range(3, last):
        route[slot] = (slot - 2, -1 if slot % 2 else 1)
    arrive, settle = {}, {}
    for first in range(1, last, 2):
        hops = (first + 1) // 2
        pair = [slot for slot in (first, first + 1) if slot in route]
        need = 2 * hops - 1
        if is_grid(chips) and hops >= SPAN:
            need = 2 * hops - 2
        for part in range(PARTS):
            after = need - 1
            if hops == 2 or not is_grid(chips) and hops == SPAN:
                after = need - 2 + part * 2 // PARTS
            if hops > SPAN:
                after = need - 2
            for slot in pair:
                arrive.setdefault(after, []).append((slot, part))
                settle.setdefault(need, []).append((slot, part))
    return route, arrive, settle


def slot_of(chunk, position, sign, chips):
    if not is_grid(chips):
        return chunk
    late = position % (chips // 2) // (chips // 4)
    ahead = (1 - 2 * late) * sign
    skipped = (SPAN + 1) - (ahead + 1) // 2
    return chunk + (chunk >= skipped).astype(jnp.int32)


def body(
    views, tok_hbm, in_gain_hbm, wq_hbm, wk_hbm, wv_hbm, wo_hbm, out_gain_hbm, list_hbm, count_hbm,
    out_ref,
    buf, wq, wk, wv, wo, in_gain, out_gain, lists, counts, qpad, kbuf, vtbuf, peak, total, acc, mask, hn, hn_in,
    load_sem, send_sem, recv_sem, pass_send, pass_recv, misc_send, misc_recv,
):
    chips = views // 2
    me = lax.axis_index("views")
    chip, core = me // 2, me % 2
    sign = 1 - 2 * core
    place = ring_position(chip, chips)
    partner = chip * 2 + 1 - core
    half = wq.shape[1]
    rows = tok_hbm.shape[0]
    heads = half // HEAD_DIM
    route, arrive, settle = ring_route(chips)

    def device(step):
        return {"views": ring_chip(place + step * sign, chips) * 2 + core}

    columns = pl.ds(pl.multiple_of(core * half, half), half)
    loads = [
        pltpu.make_async_copy(tok_hbm, buf.at[0, 0], load_sem.at[0]),
        pltpu.make_async_copy(wq_hbm.at[:, columns], wq, load_sem.at[1]),
        pltpu.make_async_copy(wk_hbm.at[:, columns], wk, load_sem.at[2]),
        pltpu.make_async_copy(wv_hbm.at[:, columns], wv, load_sem.at[3]),
        pltpu.make_async_copy(wo_hbm, wo, load_sem.at[4]),
        pltpu.make_async_copy(in_gain_hbm, in_gain, load_sem.at[5]),
        pltpu.make_async_copy(out_gain_hbm, out_gain, load_sem.at[6]),
        pltpu.make_async_copy(list_hbm, lists.at[0], load_sem.at[7]),
        pltpu.make_async_copy(count_hbm, counts.at[0], load_sem.at[8]),
    ]

    barrier = pltpu.get_barrier_semaphore()
    for way in (-1, 1):
        pl.semaphore_signal(barrier, inc=1, device_id=device(way), device_id_type=MESH)
    pl.semaphore_signal(barrier, inc=1, device_id={"views": partner}, device_id_type=MESH)
    for load in loads:
        load.start()
    pl.semaphore_wait(barrier, 3)

    size = rows // PARTS

    def hop(slot, part):
        source, step = route[slot]
        span = pl.ds(part * size, size)
        return pltpu.make_async_remote_copy(
            src_ref=tok_hbm.at[span] if source == 0 else buf.at[source, 0, span],
            dst_ref=buf.at[slot, 0, span],
            send_sem=send_sem.at[slot, part],
            recv_sem=recv_sem.at[slot, part],
            device_id=device(step),
            device_id_type=MESH,
        )

    def hand_over(slot, part):
        span = pl.ds(part * size, size)
        return pltpu.make_async_remote_copy(
            src_ref=tok_hbm.at[span] if slot == 0 else buf.at[slot, 0, span],
            dst_ref=buf.at[slot, 1, span],
            send_sem=pass_send.at[slot, part],
            recv_sem=pass_recv.at[slot, part],
            device_id={"views": partner},
            device_id_type=MESH,
        )

    list_copy = pltpu.make_async_remote_copy(
        src_ref=list_hbm, dst_ref=lists.at[1], send_sem=misc_send.at[0], recv_sem=misc_recv.at[0],
        device_id={"views": partner}, device_id_type=MESH,
    )
    count_copy = pltpu.make_async_remote_copy(
        src_ref=count_hbm, dst_ref=counts.at[1], send_sem=misc_send.at[2], recv_sem=misc_recv.at[2],
        device_id={"views": partner}, device_id_type=MESH,
    )
    swap = pltpu.make_async_remote_copy(
        src_ref=hn.at[1], dst_ref=hn_in, send_sem=misc_send.at[1], recv_sem=misc_recv.at[1],
        device_id={"views": partner}, device_id_type=MESH,
    )
    parts = range(PARTS)
    list_copy.start()
    count_copy.start()
    for part in parts:
        hand_over(0, part).start()
        for slot in route:
            if route[slot][0] == 0:
                hop(slot, part).start()

    peak[...] = jnp.full(peak.shape, -INF, jnp.float32)
    total[...] = jnp.zeros(total.shape, jnp.float32)
    acc[...] = jnp.zeros(acc.shape, jnp.float32)
    for load in loads[5:]:
        load.wait()
    list_copy.wait_recv()
    count_copy.wait_recv()
    ids = jnp.zeros((16, 1), jnp.int32)
    line = lax.broadcasted_iota(jnp.int32, (16, 1), 0)
    for t in range(CHUNKS):
        for bank in range(2):
            way = sign * (1 - 2 * bank)
            slot = slot_of(jnp.int32(t), place, way, chips)
            odd = slot % 2
            step = (slot + 1) // 2 * (2 * odd - 1) * way
            view = ring_chip(place + step, chips) * 2 + (core if bank == 0 else 1 - core)
            ids = jnp.where(line == 2 * t + bank, view, ids)
    for side, query_view in enumerate((me, partner)):
        listed = lists[side]
        valid = lax.broadcasted_iota(jnp.int32, (16, listed.shape[1]), 1) < counts[side:side + 1, :]
        hits = jnp.where(((listed == ids) | (ids == query_view)) & valid, 1.0, 0.0)
        mask[:, side * rows:(side + 1) * rows] = jnp.broadcast_to(
            jnp.max(hits, axis=1, keepdims=True), (16, rows)
        )

    def normed_of(first, second):
        raw = jnp.concatenate([buf[first, 0], buf[second, 1]], axis=0).astype(jnp.float32)
        mean_sq = jnp.mean(raw * raw, axis=-1, keepdims=True)
        return (raw * lax.rsqrt(mean_sq + 1e-6) * in_gain[...]).astype(jnp.bfloat16)

    loads[0].wait()
    for part in parts:
        hand_over(0, part).wait_recv()
    loads[1].wait()
    query = jnp.dot(normed_of(0, 0), wq[...], preferred_element_type=jnp.float32).astype(jnp.bfloat16)
    query = query.astype(jnp.float32) * HEAD_DIM ** (-0.5)
    query_t = query.T.astype(jnp.bfloat16)
    zero = jnp.zeros((HEAD_DIM, 2 * rows), jnp.bfloat16)
    for h in range(heads):
        mine = query_t[h * HEAD_DIM:(h + 1) * HEAD_DIM, :]
        qpad[h] = jnp.concatenate([mine, zero] if h % 2 == 0 else [zero, mine], axis=0)
    loads[2].wait()
    loads[3].wait()

    def chunk(slot, carry):
        for ahead_of, handed in settle.items():
            @pl.when(slot == ahead_of)
            def _(handed=handed):
                for got, part in handed:
                    hand_over(got, part).wait_recv()

        near = slot_of(slot, place, sign, chips)
        far = slot_of(slot, place, -sign, chips)
        normed = normed_of(near, far)
        kbuf[...] = jnp.dot(normed, wk[...], preferred_element_type=jnp.float32).astype(jnp.bfloat16)
        value = jnp.dot(normed, wv[...], preferred_element_type=jnp.float32)
        vtbuf[...] = value.T.astype(jnp.bfloat16)
        on_first = mask[pl.ds(2 * slot, 1), :] > 0.5
        on_second = mask[pl.ds(2 * slot + 1, 1), :] > 0.5
        def scores_of(h):
            pair = (h // 2) * 2 * HEAD_DIM
            return jnp.dot(kbuf[:, pair:pair + 2 * HEAD_DIM], qpad[h], preferred_element_type=jnp.float32)

        waiting = scores_of(0)
        pend = None
        def finish(p):
            h, keep, weights = p
            feats = slice(h * HEAD_DIM, (h + 1) * HEAD_DIM)
            acc[feats, :] = acc[feats, :] * keep + jnp.dot(vtbuf[feats, :], weights, preferred_element_type=jnp.float32)
        peaks, totals = peak[...], total[...]
        new_peaks, new_totals = [], []
        for h in range(heads):
            scores = waiting
            if h + 1 < heads:
                waiting = scores_of(h + 1)
            first, second = scores[:rows], scores[rows:]
            old = peaks[h:h + 1, :]
            new = jnp.maximum(
                jnp.where(on_first, jnp.max(first, axis=0, keepdims=True), -INF),
                jnp.where(on_second, jnp.max(second, axis=0, keepdims=True), -INF),
            )
            new = jnp.maximum(old, new)
            e_first = jnp.exp(first - jnp.where(on_first, new, INF))
            e_second = jnp.exp(second - jnp.where(on_second, new, INF))
            keep = jnp.exp(old - new)
            new_peaks.append(new)
            new_totals.append(totals[h:h + 1, :] * keep + jnp.sum(e_first + e_second, axis=0, keepdims=True))
            weights = jnp.concatenate([e_first.astype(jnp.bfloat16), e_second.astype(jnp.bfloat16)], axis=0)
            if pend is not None:
                finish(pend)
            pend = (h, keep, weights)
        finish(pend)
        peak[...] = jnp.concatenate(new_peaks, axis=0)
        total[...] = jnp.concatenate(new_totals, axis=0)

        for after, arrivals in arrive.items():
            @pl.when(slot == after)
            def _(arrivals=arrivals):
                for got, part in arrivals:
                    hop(got, part).wait_recv()
                    for later in route:
                        if route[later][0] == got:
                            hop(later, part).start()
                    hand_over(got, part).start()
        return carry

    lax.fori_loop(0, CHUNKS, chunk, 0)

    gain = out_gain[:, columns]
    pieces = []
    for h in range(heads):
        attended = acc[h * HEAD_DIM:(h + 1) * HEAD_DIM, :] / total[h:h + 1, :]
        mean_sq = jnp.mean(attended * attended, axis=0, keepdims=True)
        pieces.append(attended * lax.rsqrt(mean_sq + 1e-6))
    head_normed = (jnp.concatenate(pieces, axis=0).T * gain).astype(jnp.bfloat16)
    hn[1] = head_normed[rows:]
    swap.start()
    hn[0] = head_normed[:rows]
    loads[4].wait()
    others = pl.ds(pl.multiple_of((1 - core) * half, half), half)
    update = jnp.dot(hn[0], wo[columns, :], preferred_element_type=jnp.float32)
    swap.wait_recv()
    update = update + jnp.dot(hn_in[...], wo[others, :], preferred_element_type=jnp.float32)
    out_ref[...] = (buf[0, 0].astype(jnp.float32) + update).astype(out_ref.dtype)

    for part in parts:
        for slot in route:
            hop(slot, part).wait_send()
        for slot in range(len(route) + 1):
            hand_over(slot, part).wait_send()
    list_copy.wait_send()
    count_copy.wait_send()
    swap.wait_send()


def on_device(tokens, in_gain, w_query, w_key, w_value, w_out, out_gain, covis_list, covis_count):
    views = lax.axis_size("views")
    rows, width = tokens.shape[1:]
    half = width // 2
    slots = len(ring_route(views // 2)[0]) + 1
    slots_listed = covis_list.shape[1]
    hbm = pl.BlockSpec(memory_space=pltpu.HBM)
    vmem = pl.BlockSpec(memory_space=pltpu.VMEM)
    bf16, f32 = jnp.bfloat16, jnp.float32
    heads = half // HEAD_DIM
    dma = pltpu.SemaphoreType.DMA
    out = pl.pallas_call(
        functools.partial(body, views),
        out_shape=jax.ShapeDtypeStruct((rows, width), tokens.dtype),
        in_specs=[hbm] * 9,
        out_specs=vmem,
        scratch_shapes=[
            pltpu.VMEM((slots, 2, rows, width), bf16),
            pltpu.VMEM((width, half), bf16),
            pltpu.VMEM((width, half), bf16),
            pltpu.VMEM((width, half), bf16),
            pltpu.VMEM((width, width), bf16),
            pltpu.VMEM((1, width), f32),
            pltpu.VMEM((1, width), f32),
            pltpu.VMEM((2, 1, slots_listed), jnp.int32),
            pltpu.VMEM((2, 1), jnp.int32),
            pltpu.VMEM((heads, 2 * HEAD_DIM, 2 * rows), bf16),
            pltpu.VMEM((2 * rows, half), bf16),
            pltpu.VMEM((half, 2 * rows), bf16),
            pltpu.VMEM((heads, 2 * rows), f32),
            pltpu.VMEM((heads, 2 * rows), f32),
            pltpu.VMEM((half, 2 * rows), f32),
            pltpu.VMEM((16, 2 * rows), f32),
            pltpu.VMEM((2, rows, half), bf16),
            pltpu.VMEM((rows, half), bf16),
            dma((9,)),
            dma((slots, PARTS)),
            dma((slots, PARTS)),
            dma((slots, PARTS)),
            dma((slots, PARTS)),
            dma((3,)),
            dma((3,)),
        ],
        compiler_params=pltpu.CompilerParams(
            collective_id=0, has_side_effects=True, vmem_limit_bytes=60 * 1024 * 1024
        ),
    )(tokens[0], in_gain[None], w_query, w_key, w_value, w_out, out_gain[None], covis_list, covis_count)
    return out[None]


def solution(mesh):
    in_specs = (
        P(("groups", "views"), None, None),
        P(), P(), P(), P(), P(), P(),
        P(("groups", "views"), None),
        P(("groups", "views")),
    )
    out_specs = P(("groups", "views"), None, None)
    return jax.shard_map(on_device, mesh=mesh, in_specs=in_specs, out_specs=out_specs, check_vma=False)
```

profile of v0, /device:TPU:1, one launch (start us, length us, event | category | flops | bytes accessed | tf_op | source)
XLA Modules:
  0.0 36.3 jit_solution(953144657320117888)
XLA Ops:
  0.7 34.0 %shard_map.91 = bf16[128,1024]{1,0:T(8,128)(2,1)} custom-call(bf16[128,1024]{1,0:T(8,128)(2,1)} %bitcast.5, f32[1,1024]{1,0:T(1,128)} %bitcast.6, bf16[1024,1024]{1,0:T(8,128)(2,1)} %wq_hbm.1, bf16[1024,1024]{1,0:T(8,128)(2,1)} %wk_hbm.1, bf16[1024,1024]{1,0:T(8,128)(2,1)} %wv_hbm.1, bf16[1024,1024]{1,0:T(8,128)(2,1)} %wo_hbm.1, f32[1,1024]{1,0:T(1,128)} %bitcast.7, ...), custom_call_target="tpu_custom_call" | custom-call | tf_op jit(solution)/shard_map/pallas_call | solution.py:306
  34.7 1.7 %copy.12 = bf16[1,128,1024]{2,1,0:T(8,128)(2,1)} copy(bf16[1,128,1024]{2,1,0:T(8,128)(2,1)} %bitcast.4) | data formatting | bytes 524288
where the time goes:
time: 36.5 us; the launch traced here: 36.3 us
  Pallas kernels  34 us (93%)
  local copies, waits for them, and re-layouts  1.67 us (5%)
  between operations  0.66 us (2%)
    pallas_call x1, Pallas kernels, on_device(): pl.pallas_call(functools.partial(body, views), out_shape=jax.ShapeDtypeSt...  34 us
    unnamed x1, local copies, waits for them, and re-layouts  1.67 us

commit v1 on v0

v1 whole, which is shorter than its diff:
```python
import functools

import jax
import jax.numpy as jnp
from jax import lax
from jax.experimental import pallas as pl
from jax.experimental.pallas import tpu as pltpu
from jax.sharding import PartitionSpec as P

HEADS = 16
HEAD_DIM = 64
REACH = 6
SPAN = REACH // 2
SLOTS = 2 * SPAN + 2
RELAY = SLOTS - 1
PARTS = 4
ROUNDS = SPAN * PARTS
MESH = pl.DeviceIdType.MESH
INF = float("inf")
LOW = -3e38


def is_grid(chips):
    return chips == 2 * SPAN + 2


def grid_chip(chip, mirror, depth, side):
    z, y = chip // 2, chip % 2
    if depth:
        z = z + 1 - 2 * (z % 2)
    if mirror:
        z = 3 - z
    if side:
        y = 1 - y
    return 2 * z + y


OUTER_SLOTS = ((0, 0, 0), (0, 1, 0), (0, 0, 1), (1, 0, 0), (0, 1, 1), (1, 1, 1), (1, 0, 1))
INNER_SLOTS = ((0, 0, 0), (0, 1, 0), (0, 0, 1), (0, 1, 1), (1, 1, 1), (1, 0, 1), (1, 0, 0))
INNER_STEPS = ((0, 0, 0, 1), (2, 0, 2, 1), (1, 0, 4, 0), (1, 1, 4, 1), (5, 0, 5, 1), (3, 0, 6, 0), (3, 1, 6, 1))
OUTER_STEPS = ((0, 0, 0, 1),) + tuple(
    (1 + 2 * group, late, 2 + 2 * group, late) for group in range(SPAN) for late in range(2)
)


def slot_chips(chip, chips):
    if is_grid(chips):
        outer = (chip // 2) % 3 == 0
        return [
            jnp.where(outer, grid_chip(chip, *far), grid_chip(chip, *near))
            for far, near in zip(OUTER_SLOTS, INNER_SLOTS)
        ]
    found = [chip]
    for hops in range(1, SPAN + 1):
        found += [(chip - hops + chips) % chips, (chip + hops) % chips]
    return found


def body(
    views, tok_hbm, in_gain_hbm, wq_hbm, wk_hbm, wv_hbm, wo_hbm, out_gain_hbm, list_hbm, count_hbm,
    out_ref,
    buf, other, wq, wk, wv, wo, in_gain, out_gain, lists, counts, qpad, kbuf, vtbuf, stats, acc, mask,
    stats_in, acc_in,
    load_sem, send_sem, recv_sem, misc_send, misc_recv,
):
    chips = views // 2
    grid = is_grid(chips)
    me = lax.axis_index("views")
    chip, core = me // 2, me % 2
    partner = chip * 2 + 1 - core
    rows, width = tok_hbm.shape
    heads = width // HEAD_DIM
    size = rows // PARTS
    half = rows // 2
    steps = ROUNDS // 2

    loads = [
        pltpu.make_async_copy(tok_hbm, buf.at[0], load_sem.at[0]),
        pltpu.make_async_copy(in_gain_hbm, in_gain, load_sem.at[5]),
        pltpu.make_async_copy(list_hbm, lists.at[0], load_sem.at[7]),
        pltpu.make_async_copy(count_hbm, counts.at[0], load_sem.at[8]),
        pltpu.make_async_copy(wq_hbm, wq, load_sem.at[1]),
        pltpu.make_async_copy(wk_hbm, wk, load_sem.at[2]),
        pltpu.make_async_copy(wv_hbm, wv, load_sem.at[3]),
        pltpu.make_async_copy(out_gain_hbm, out_gain, load_sem.at[6]),
        pltpu.make_async_copy(wo_hbm, wo, load_sem.at[4]),
    ]

    if grid:
        outer = (chip // 2) % 3 == 0
        beside = grid_chip(chip, 0, 0, 1) * 2 + core
        along = grid_chip(chip, 0, 1, 0) * 2 + core
        across = grid_chip(chip, 1, 0, 0) * 2 + core
        skip = grid_chip(chip, 1, 1, 0) * 2 + core
    else:
        outer = None
        beside = (chip + chips - 1) % chips * 2 + core
        along = (chip + 1) % chips * 2 + core

    barrier = pltpu.get_barrier_semaphore()
    for device in (partner, beside, along):
        pl.semaphore_signal(barrier, inc=1, device_id={"views": device}, device_id_type=MESH)
    if grid:
        @pl.when(jnp.logical_not(outer))
        def _():
            for device in (across, skip):
                pl.semaphore_signal(barrier, inc=1, device_id={"views": device}, device_id_type=MESH)
    for load in loads:
        load.start()
    pl.semaphore_wait(barrier, 4 if grid else 3)

    def send(kind, source, slot, part, device):
        span = pl.ds(pl.multiple_of(part * size, size), size)
        return pltpu.make_async_remote_copy(
            src_ref=tok_hbm.at[span] if source is None else buf.at[source, span],
            dst_ref=buf.at[slot, span],
            send_sem=send_sem.at[kind, part],
            recv_sem=recv_sem.at[slot, part],
            device_id={"views": device},
            device_id_type=MESH,
        )

    def arrived(slot, part):
        send(0, slot, slot, part, partner).wait_recv()

    def partner_copy(src, dst, index):
        return pltpu.make_async_remote_copy(
            src_ref=src, dst_ref=dst, send_sem=misc_send.at[index], recv_sem=misc_recv.at[index],
            device_id={"views": partner}, device_id_type=MESH,
        )

    first_copies = [
        partner_copy(tok_hbm, other, 0),
        partner_copy(list_hbm, lists.at[1], 1),
        partner_copy(count_hbm, counts.at[1], 2),
    ]
    if grid:
        @pl.when(outer)
        def _():
            for part in range(PARTS):
                send(0, None, RELAY, part, skip).start()
                send(2, None, 2, part, beside).start()
            for part in range(PARTS):
                send(1, None, 1, part, along).start()

        @pl.when(jnp.logical_not(outer))
        def _():
            for part in range(PARTS):
                send(0, None, 1, part, along).start()
                send(1, None, 2, part, beside).start()
    else:
        for part in range(PARTS):
            send(0, None, 1, part, along).start()
            send(1, None, 2, part, beside).start()
    for copy in first_copies:
        copy.start()

    def ring_poll(r):
        group, part = r // PARTS, r % PARTS
        arrived(1 + 2 * group, part)
        arrived(2 + 2 * group, part)

        @pl.when(group < SPAN - 1)
        def _():
            send(2 + 2 * group, 1 + 2 * group, 3 + 2 * group, part, along).start()
            send(3 + 2 * group, 2 + 2 * group, 4 + 2 * group, part, beside).start()

    def outer_poll(r):
        group, part = r // PARTS, r % PARTS
        arrived(1 + 2 * group, part)

        @pl.when(group < 2)
        def _():
            send(3 + group, 1 + 2 * group, 4 + 2 * group, part, beside).start()
        arrived(2 + 2 * group, part)

        @pl.when(group == 0)
        def _():
            send(5, 2, 3, part, along).start()

    def far_on(part):
        arrived(RELAY, part)
        send(3, RELAY, 3, part, along).start()
        send(4, RELAY, 4, part, beside).start()

    def corner_on(part):
        arrived(5, part)
        send(5, 5, 5, part, along).start()

    def inner_poll(r):
        if r < PARTS:
            arrived(2, r)
        if 1 <= r < 5:
            far_on(r - 1)
        if r == 2:
            for part in range(3):
                send(6, 2, 5, part, across).start()
        if r == 3:
            send(6, 2, 5, 3, across).start()
            for part in range(PARTS):
                send(2, None, 6, part, across).start()
        if 5 <= r < 9:
            corner_on(r - 5)
        if 4 <= r < 8:
            arrived(1, r - 4)
            arrived(4, r - 4)
        if 8 <= r < 12:
            arrived(3, r - 8)
        if 9 <= r:
            arrived(6, r - 9)

    inner_polls = {
        0: ((0,), (1, 2, 3)), 1: ((4,), (5,)), 2: ((6,), (7,)), 3: ((8,), ()), 4: ((9,), (10,)), 5: ((11,), (12,)),
    }

    def poll(j, second):
        if not grid:
            @pl.when(j < steps)
            def _():
                ring_poll(2 * j + second)
            return

        @pl.when(jnp.logical_and(outer, j < steps))
        def _():
            outer_poll(2 * j + second)

        @pl.when(jnp.logical_not(outer))
        def _():
            for at, polls in inner_polls.items():
                if polls[second]:
                    @pl.when(j == at)
                    def _(polls=polls):
                        for r in polls[second]:
                            inner_poll(r)

    stats[:, 0] = jnp.full((heads, 2 * rows), LOW, jnp.float32)
    stats[:, 1] = jnp.zeros((heads, 2 * rows), jnp.float32)
    acc[...] = jnp.zeros(acc.shape, jnp.float32)
    for load in loads[:4]:
        load.wait()

    def normed_of(raw):
        raw = raw.astype(jnp.float32)
        mean_sq = jnp.mean(raw * raw, axis=-1, keepdims=True)
        return (raw * lax.rsqrt(mean_sq + 1e-6) * in_gain[...]).astype(jnp.bfloat16)

    for copy in first_copies:
        copy.wait_recv()
    ids = jnp.zeros((8, 1), jnp.int32)
    line = lax.broadcasted_iota(jnp.int32, (8, 1), 0)
    for slot, at in enumerate(slot_chips(chip, chips)):
        ids = jnp.where(line == slot, at * 2 + core, ids)
    for side, query_view in enumerate((me, partner)):
        listed = lists[side]
        valid = lax.broadcasted_iota(jnp.int32, (8, listed.shape[1]), 1) < counts[side:side + 1, :]
        hits = jnp.where(((listed == ids) | (ids == query_view)) & valid, 1.0, 0.0)
        mask[:, side * rows:(side + 1) * rows] = jnp.broadcast_to(
            jnp.max(hits, axis=1, keepdims=True), (8, rows)
        )

    loads[4].wait()
    query_in = jnp.concatenate([normed_of(buf[0]), normed_of(other[...])], axis=0)
    query = jnp.dot(query_in, wq[...], preferred_element_type=jnp.float32).astype(jnp.bfloat16)
    query = query.astype(jnp.float32) * HEAD_DIM ** (-0.5)
    query_t = query.T.astype(jnp.bfloat16)
    zero = jnp.zeros((HEAD_DIM, 2 * rows), jnp.bfloat16)
    for h in range(heads):
        mine = query_t[h * HEAD_DIM:(h + 1) * HEAD_DIM, :]
        qpad[h] = jnp.concatenate([mine, zero] if h % 2 == 0 else [zero, mine], axis=0)
    loads[5].wait()
    loads[6].wait()

    def project(first, second):
        normed = normed_of(jnp.concatenate([first, second], axis=0))
        kbuf[...] = jnp.dot(normed, wk[...], preferred_element_type=jnp.float32).astype(jnp.bfloat16)
        value = jnp.dot(normed, wv[...], preferred_element_type=jnp.float32)
        vtbuf[...] = value.T.astype(jnp.bfloat16)

    def attend(near, far):
        on_first = mask[pl.ds(near, 1), :] > 0.5
        on_second = mask[pl.ds(far, 1), :] > 0.5
        keys = kbuf.shape[0] // 2

        def scores_of(h):
            pair = (h // 2) * 2 * HEAD_DIM
            return jnp.dot(kbuf[:, pair:pair + 2 * HEAD_DIM], qpad[h], preferred_element_type=jnp.float32)

        def finish(p):
            h, keep, weights = p
            feats = slice(h * HEAD_DIM, (h + 1) * HEAD_DIM)
            acc[feats, :] = acc[feats, :] * keep + jnp.dot(vtbuf[feats, :], weights, preferred_element_type=jnp.float32)

        waiting = scores_of(0)
        pend = None
        for h in range(heads):
            scores = waiting
            if h + 1 < heads:
                waiting = scores_of(h + 1)
            first, second = scores[:keys], scores[keys:]
            old = stats[h, 0:1, :]
            new = jnp.maximum(
                jnp.where(on_first, jnp.max(first, axis=0, keepdims=True), -INF),
                jnp.where(on_second, jnp.max(second, axis=0, keepdims=True), -INF),
            )
            new = jnp.maximum(old, new)
            e_first = jnp.exp(first - jnp.where(on_first, new, INF))
            e_second = jnp.exp(second - jnp.where(on_second, new, INF))
            keep = jnp.exp(old - new)
            stats[h, 0:1, :] = new
            stats[h, 1:2, :] = stats[h, 1:2, :] * keep + jnp.sum(e_first + e_second, axis=0, keepdims=True)
            weights = jnp.concatenate([e_first.astype(jnp.bfloat16), e_second.astype(jnp.bfloat16)], axis=0)
            if pend is not None:
                finish(pend)
            pend = (h, keep, weights)
        finish(pend)

    def pick(table, j):
        found = table[0]
        for at in range(1, len(table)):
            found = jnp.where(j == at, table[at], found)
        return found

    def step(j, carry):
        if grid:
            picks = [
                jnp.where(outer, pick(far, j), pick(near, j))
                for far, near in zip(zip(*OUTER_STEPS), zip(*INNER_STEPS))
            ]
        else:
            picks = [pick(column, j) for column in zip(*OUTER_STEPS)]
        near, near_half, far, far_half = picks
        near_row = pl.multiple_of(near_half * half, half)
        far_row = pl.multiple_of(far_half * half, half)
        project(buf[near, pl.ds(near_row, half)], buf[far, pl.ds(far_row, half)])
        poll(j, 0)
        attend(near, far)
        poll(j, 1)
        return carry

    lax.fori_loop(0, steps + 1, step, 0)

    swaps = [
        partner_copy(stats.at[:, :, pl.ds(rows, rows)], stats_in, 3),
        partner_copy(acc.at[:, pl.ds(rows, rows)], acc_in, 4),
    ]
    for swap in swaps:
        swap.start()
    loads[7].wait()
    loads[8].wait()
    for swap in swaps:
        swap.wait_recv()
    gain = out_gain[...]
    pieces = []
    for h in range(heads):
        feats = slice(h * HEAD_DIM, (h + 1) * HEAD_DIM)
        peak, peak_in = stats[h, 0:1, :rows], stats_in[h, 0:1, :]
        new = jnp.maximum(peak, peak_in)
        keep, keep_in = jnp.exp(peak - new), jnp.exp(peak_in - new)
        total = stats[h, 1:2, :rows] * keep + stats_in[h, 1:2, :] * keep_in
        attended = (acc[feats, :rows] * keep + acc_in[feats, :] * keep_in) / total
        mean_sq = jnp.mean(attended * attended, axis=0, keepdims=True)
        pieces.append(attended * lax.rsqrt(mean_sq + 1e-6))
    head_normed = (jnp.concatenate(pieces, axis=0).T * gain).astype(jnp.bfloat16)
    update = jnp.dot(head_normed, wo[...], preferred_element_type=jnp.float32)
    out_ref[...] = (buf[0].astype(jnp.float32) + update).astype(out_ref.dtype)

    for part in range(PARTS):
        for kind in range(6):
            send(kind, None, 1, part, partner).wait_send()
        if grid:
            @pl.when(jnp.logical_not(outer))
            def _(part=part):
                send(6, None, 1, part, partner).wait_send()
    for copy in first_copies + swaps:
        copy.wait_send()


def on_device(tokens, in_gain, w_query, w_key, w_value, w_out, out_gain, covis_list, covis_count):
    views = lax.axis_size("views")
    rows, width = tokens.shape[1:]
    slots_listed = covis_list.shape[1]
    hbm = pl.BlockSpec(memory_space=pltpu.HBM)
    vmem = pl.BlockSpec(memory_space=pltpu.VMEM)
    bf16, f32 = jnp.bfloat16, jnp.float32
    heads = width // HEAD_DIM
    dma = pltpu.SemaphoreType.DMA
    out = pl.pallas_call(
        functools.partial(body, views),
        out_shape=jax.ShapeDtypeStruct((rows, width), tokens.dtype),
        in_specs=[hbm] * 9,
        out_specs=vmem,
        scratch_shapes=[
            pltpu.VMEM((SLOTS, rows, width), bf16),
            pltpu.VMEM((rows, width), bf16),
            pltpu.VMEM((width, width), bf16),
            pltpu.VMEM((width, width), bf16),
            pltpu.VMEM((width, width), bf16),
            pltpu.VMEM((width, width), bf16),
            pltpu.VMEM((1, width), f32),
            pltpu.VMEM((1, width), f32),
            pltpu.VMEM((2, 1, slots_listed), jnp.int32),
            pltpu.VMEM((2, 1), jnp.int32),
            pltpu.VMEM((heads, 2 * HEAD_DIM, 2 * rows), bf16),
            pltpu.VMEM((rows, width), bf16),
            pltpu.VMEM((width, rows), bf16),
            pltpu.VMEM((heads, 2, 2 * rows), f32),
            pltpu.VMEM((width, 2 * rows), f32),
            pltpu.VMEM((8, 2 * rows), f32),
            pltpu.VMEM((heads, 2, rows), f32),
            pltpu.VMEM((width, rows), f32),
            dma((9,)),
            dma((8, PARTS)),
            dma((SLOTS, PARTS)),
            dma((5,)),
            dma((5,)),
        ],
        compiler_params=pltpu.CompilerParams(
            collective_id=0, has_side_effects=True, vmem_limit_bytes=60 * 1024 * 1024
        ),
    )(tokens[0], in_gain[None], w_query, w_key, w_value, w_out, out_gain[None], covis_list, covis_count)
    return out[None]


def solution(mesh):
    in_specs = (
        P(("groups", "views"), None, None),
        P(), P(), P(), P(), P(), P(),
        P(("groups", "views"), None),
        P(("groups", "views")),
    )
    out_specs = P(("groups", "views"), None, None)
    return jax.shard_map(on_device, mesh=mesh, in_specs=in_specs, out_specs=out_specs, check_vma=False)
```

time: 36.5 us -> 33.6 us (0.921)
  the two profiles are of different devices: /device:TPU:1 before, /device:TPU:17 now
where the time goes in v1:
time: 33.6 us; the launch traced here: 33.5 us
  Pallas kernels  31.1 us (93%)
  local copies, waits for them, and re-layouts  1.67 us (5%)
  between operations  0.66 us (2%)
    pallas_call x1, Pallas kernels, on_device(): pl.pallas_call(functools.partial(body, views), out_shape=jax.ShapeDtypeSt...  31.1 us
    unnamed x1, local copies, waits for them, and re-layouts  1.67 us

profile of v1, /device:TPU:17, one launch (start us, length us, event | category | flops | bytes accessed | tf_op | source)
XLA Modules:
  0.0 33.5 jit_solution(857178827545250195)
XLA Ops:
  0.7 31.1 %shard_map.91 = bf16[128,1024]{1,0:T(8,128)(2,1)} custom-call(bf16[128,1024]{1,0:T(8,128)(2,1)} %bitcast.5, f32[1,1024]{1,0:T(1,128)} %bitcast.6, bf16[1024,1024]{1,0:T(8,128)(2,1)} %wq_hbm.1, bf16[1024,1024]{1,0:T(8,128)(2,1)} %wk_hbm.1, bf16[1024,1024]{1,0:T(8,128)(2,1)} %wv_hbm.1, bf16[1024,1024]{1,0:T(8,128)(2,1)} %wo_hbm.1, f32[1,1024]{1,0:T(1,128)} %bitcast.7, ...), custom_call_target="tpu_custom_call" | custom-call | tf_op jit(solution)/shard_map/pallas_call | solution.py:387
  31.8 1.7 %copy.12 = bf16[1,128,1024]{2,1,0:T(8,128)(2,1)} copy(bf16[1,128,1024]{2,1,0:T(8,128)(2,1)} %bitcast.4) | data formatting | bytes 524288

commit v2 on v1

--- a/solution.py
+++ b/solution.py
@@ -15,6 +15,7 @@
 RELAY = SLOTS - 1
 PARTS = 4
 ROUNDS = SPAN * PARTS
+GROUP = 4
 MESH = pl.DeviceIdType.MESH
 INF = float("inf")
 LOW = -3e38
@@ -59,8 +60,8 @@
 def body(
     views, tok_hbm, in_gain_hbm, wq_hbm, wk_hbm, wv_hbm, wo_hbm, out_gain_hbm, list_hbm, count_hbm,
     out_ref,
-    buf, other, wq, wk, wv, wo, in_gain, out_gain, lists, counts, qpad, kbuf, vtbuf, stats, acc, mask,
-    stats_in, acc_in,
+    buf, other, wq, wk, wv, wo, in_gain, out_gain, lists, counts, qpad, kbuf, vtbuf,
+    peaks, totals, acc, mask, stats_out, stats_in, acc_in,
     load_sem, send_sem, recv_sem, misc_send, misc_recv,
 ):
     chips = views // 2
@@ -73,6 +74,7 @@
     size = rows // PARTS
     half = rows // 2
     steps = ROUNDS // 2
+    groups = heads // GROUP
 
     loads = [
         pltpu.make_async_copy(tok_hbm, buf.at[0], load_sem.at[0]),
@@ -214,13 +216,14 @@
     }
 
     def poll(j, second):
+        ahead = j < steps
         if not grid:
-            @pl.when(j < steps)
+            @pl.when(ahead)
             def _():
                 ring_poll(2 * j + second)
             return
 
-        @pl.when(jnp.logical_and(outer, j < steps))
+        @pl.when(jnp.logical_and(outer, ahead))
         def _():
             outer_poll(2 * j + second)
 
@@ -233,8 +236,8 @@
                         for r in polls[second]:
                             inner_poll(r)
 
-    stats[:, 0] = jnp.full((heads, 2 * rows), LOW, jnp.float32)
-    stats[:, 1] = jnp.zeros((heads, 2 * rows), jnp.float32)
+    peaks[...] = jnp.full(peaks.shape, LOW, jnp.float32)
+    totals[...] = jnp.zeros(totals.shape, jnp.float32)
     acc[...] = jnp.zeros(acc.shape, jnp.float32)
     for load in loads[:4]:
         load.wait()
@@ -254,9 +257,9 @@
         listed = lists[side]
         valid = lax.broadcasted_iota(jnp.int32, (8, listed.shape[1]), 1) < counts[side:side + 1, :]
         hits = jnp.where(((listed == ids) | (ids == query_view)) & valid, 1.0, 0.0)
-        mask[:, side * rows:(side + 1) * rows] = jnp.broadcast_to(
-            jnp.max(hits, axis=1, keepdims=True), (8, rows)
-        )
+        hit = jnp.max(hits, axis=1, keepdims=True)
+        for slot in range(SLOTS):
+            mask[slot, :, side * rows:(side + 1) * rows] = jnp.broadcast_to(hit[slot:slot + 1], (8, rows))
 
     loads[4].wait()
     query_in = jnp.concatenate([normed_of(buf[0]), normed_of(other[...])], axis=0)
@@ -270,25 +273,32 @@
     loads[5].wait()
     loads[6].wait()
 
-    def project(first, second):
+    def project(first, second, keys, values):
         normed = normed_of(jnp.concatenate([first, second], axis=0))
-        kbuf[...] = jnp.dot(normed, wk[...], preferred_element_type=jnp.float32).astype(jnp.bfloat16)
+        keys[...] = jnp.dot(normed, wk[...], preferred_element_type=jnp.float32).astype(jnp.bfloat16)
         value = jnp.dot(normed, wv[...], preferred_element_type=jnp.float32)
-        vtbuf[...] = value.T.astype(jnp.bfloat16)
-
-    def attend(near, far):
-        on_first = mask[pl.ds(near, 1), :] > 0.5
-        on_second = mask[pl.ds(far, 1), :] > 0.5
-        keys = kbuf.shape[0] // 2
+        values[...] = value.T.astype(jnp.bfloat16)
+
+    def attend(near, far, keys, values, handed=None):
+        on_first, on_second = mask[near] > 0.5, mask[far] > 0.5
+        span = keys.shape[0]
+        tiles = span // 16
+        queries = 2 * rows
 
         def scores_of(h):
             pair = (h // 2) * 2 * HEAD_DIM
-            return jnp.dot(kbuf[:, pair:pair + 2 * HEAD_DIM], qpad[h], preferred_element_type=jnp.float32)
+            scores = jnp.dot(keys[:, pair:pair + 2 * HEAD_DIM], qpad[h], preferred_element_type=jnp.float32)
+            return scores.reshape(2 * tiles, 8, queries)
 
         def finish(p):
             h, keep, weights = p
             feats = slice(h * HEAD_DIM, (h + 1) * HEAD_DIM)
-            acc[feats, :] = acc[feats, :] * keep + jnp.dot(vtbuf[feats, :], weights, preferred_element_type=jnp.float32)
+            kept = acc[feats, :].reshape(HEAD_DIM // 8, 8, queries) * keep[None]
+            acc[feats, :] = kept.reshape(HEAD_DIM, queries) + jnp.dot(
+                values[feats, :], weights, preferred_element_type=jnp.float32
+            )
+            if handed is not None and (h + 1) % GROUP == 0:
+                handed(h // GROUP)
 
         waiting = scores_of(0)
         pend = None
@@ -296,19 +306,19 @@
             scores = waiting
             if h + 1 < heads:
                 waiting = scores_of(h + 1)
-            first, second = scores[:keys], scores[keys:]
-            old = stats[h, 0:1, :]
+            first, second = scores[:tiles], scores[tiles:]
+            old = peaks[h]
             new = jnp.maximum(
-                jnp.where(on_first, jnp.max(first, axis=0, keepdims=True), -INF),
-                jnp.where(on_second, jnp.max(second, axis=0, keepdims=True), -INF),
+                jnp.where(on_first, jnp.max(first, axis=0), -INF),
+                jnp.where(on_second, jnp.max(second, axis=0), -INF),
             )
-            new = jnp.maximum(old, new)
-            e_first = jnp.exp(first - jnp.where(on_first, new, INF))
-            e_second = jnp.exp(second - jnp.where(on_second, new, INF))
+            new = jnp.maximum(old, jnp.broadcast_to(jnp.max(new, axis=0, keepdims=True), (8, queries)))
+            e_first = jnp.exp(first - jnp.where(on_first, new, INF)[None])
+            e_second = jnp.exp(second - jnp.where(on_second, new, INF)[None])
             keep = jnp.exp(old - new)
-            stats[h, 0:1, :] = new
-            stats[h, 1:2, :] = stats[h, 1:2, :] * keep + jnp.sum(e_first + e_second, axis=0, keepdims=True)
-            weights = jnp.concatenate([e_first.astype(jnp.bfloat16), e_second.astype(jnp.bfloat16)], axis=0)
+            peaks[h] = new
+            totals[h] = totals[h] * keep + (jnp.sum(e_first, axis=0) + jnp.sum(e_second, axis=0))
+            weights = jnp.concatenate([e_first, e_second], axis=0).reshape(span, queries).astype(jnp.bfloat16)
             if pend is not None:
                 finish(pend)
             pend = (h, keep, weights)
@@ -331,38 +341,60 @@
         near, near_half, far, far_half = picks
         near_row = pl.multiple_of(near_half * half, half)
         far_row = pl.multiple_of(far_half * half, half)
-        project(buf[near, pl.ds(near_row, half)], buf[far, pl.ds(far_row, half)])
+        project(buf[near, pl.ds(near_row, half)], buf[far, pl.ds(far_row, half)], kbuf, vtbuf)
         poll(j, 0)
-        attend(near, far)
+        attend(near, far, kbuf, vtbuf)
         poll(j, 1)
         return carry
 
-    lax.fori_loop(0, steps + 1, step, 0)
-
-    swaps = [
-        partner_copy(stats.at[:, :, pl.ds(rows, rows)], stats_in, 3),
-        partner_copy(acc.at[:, pl.ds(rows, rows)], acc_in, 4),
-    ]
-    for swap in swaps:
-        swap.start()
+    lax.fori_loop(0, steps, step, 0)
+
+    def stats_swap(group):
+        return partner_copy(stats_out.at[group], stats_in.at[group], 3 + group)
+
+    def acc_swap(group):
+        feats = pl.ds(group * GROUP * HEAD_DIM, GROUP * HEAD_DIM)
+        return partner_copy(acc.at[feats, pl.ds(rows, rows)], acc_in.at[feats], 3 + groups + group)
+
+    def totals_of(h, side):
+        return jnp.sum(totals[h][:, side * rows:(side + 1) * rows], axis=0, keepdims=True)
+
+    def hand(group):
+        acc_swap(group).start()
+        members = range(group * GROUP, (group + 1) * GROUP)
+        stats_out[group] = jnp.concatenate(
+            [peaks[h][:1, rows:] for h in members] + [totals_of(h, 1) for h in members], axis=0
+        )
+        stats_swap(group).start()
+
+    if grid:
+        near, far = (jnp.where(outer, OUTER_STEPS[-1][at], INNER_STEPS[-1][at]) for at in (0, 2))
+    else:
+        near, far = (jnp.int32(OUTER_STEPS[-1][at]) for at in (0, 2))
+    span = pl.ds(half, half)
+    project(buf[near, span], buf[far, span], kbuf, vtbuf)
+    attend(near, far, kbuf, vtbuf, hand)
+
     loads[7].wait()
     loads[8].wait()
-    for swap in swaps:
-        swap.wait_recv()
-    gain = out_gain[...]
-    pieces = []
-    for h in range(heads):
-        feats = slice(h * HEAD_DIM, (h + 1) * HEAD_DIM)
-        peak, peak_in = stats[h, 0:1, :rows], stats_in[h, 0:1, :]
-        new = jnp.maximum(peak, peak_in)
-        keep, keep_in = jnp.exp(peak - new), jnp.exp(peak_in - new)
-        total = stats[h, 1:2, :rows] * keep + stats_in[h, 1:2, :] * keep_in
-        attended = (acc[feats, :rows] * keep + acc_in[feats, :] * keep_in) / total
-        mean_sq = jnp.mean(attended * attended, axis=0, keepdims=True)
-        pieces.append(attended * lax.rsqrt(mean_sq + 1e-6))
-    head_normed = (jnp.concatenate(pieces, axis=0).T * gain).astype(jnp.bfloat16)
-    update = jnp.dot(head_normed, wo[...], preferred_element_type=jnp.float32)
-    out_ref[...] = (buf[0].astype(jnp.float32) + update).astype(out_ref.dtype)
+    update = buf[0].astype(jnp.float32)
+    for group in range(groups):
+        stats_swap(group).wait_recv()
+        acc_swap(group).wait_recv()
+        pieces = []
+        for at, h in enumerate(range(group * GROUP, (group + 1) * GROUP)):
+            feats = slice(h * HEAD_DIM, (h + 1) * HEAD_DIM)
+            peak, peak_in = peaks[h][:1, :rows], stats_in[group, at:at + 1, :]
+            new = jnp.maximum(peak, peak_in)
+            keep, keep_in = jnp.exp(peak - new), jnp.exp(peak_in - new)
+            total = totals_of(h, 0) * keep + stats_in[group, GROUP + at:GROUP + at + 1, :] * keep_in
+            attended = (acc[feats, :rows] * keep + acc_in[feats, :] * keep_in) / total
+            mean_sq = jnp.mean(attended * attended, axis=0, keepdims=True)
+            pieces.append(attended * lax.rsqrt(mean_sq + 1e-6))
+        feats = slice(group * GROUP * HEAD_DIM, (group + 1) * GROUP * HEAD_DIM)
+        head_normed = (jnp.concatenate(pieces, axis=0).T * out_gain[:, feats]).astype(jnp.bfloat16)
+        update = update + jnp.dot(head_normed, wo[feats, :], preferred_element_type=jnp.float32)
+    out_ref[...] = update.astype(out_ref.dtype)
 
     for part in range(PARTS):
         for kind in range(6):
@@ -371,8 +403,11 @@
             @pl.when(jnp.logical_not(outer))
             def _(part=part):
                 send(6, None, 1, part, partner).wait_send()
-    for copy in first_copies + swaps:
+    for copy in first_copies:
         copy.wait_send()
+    for group in range(groups):
+        stats_swap(group).wait_send()
+        acc_swap(group).wait_send()
 
 
 def on_device(tokens, in_gain, w_query, w_key, w_value, w_out, out_gain, covis_list, covis_count):
@@ -403,21 +438,23 @@
             pltpu.VMEM((heads, 2 * HEAD_DIM, 2 * rows), bf16),
             pltpu.VMEM((rows, width), bf16),
             pltpu.VMEM((width, rows), bf16),
-            pltpu.VMEM((heads, 2, 2 * rows), f32),
+            pltpu.VMEM((heads, 8, 2 * rows), f32),
+            pltpu.VMEM((heads, 8, 2 * rows), f32),
             pltpu.VMEM((width, 2 * rows), f32),
-            pltpu.VMEM((8, 2 * rows), f32),
-            pltpu.VMEM((heads, 2, rows), f32),
+            pltpu.VMEM((SLOTS, 8, 2 * rows), f32),
+            pltpu.VMEM((heads // GROUP, 2 * GROUP, rows), f32),
+            pltpu.VMEM((heads // GROUP, 2 * GROUP, rows), f32),
             pltpu.VMEM((width, rows), f32),
             dma((9,)),
             dma((8, PARTS)),
             dma((SLOTS, PARTS)),
-            dma((5,)),
-            dma((5,)),
+            dma((3 + 2 * (heads // GROUP),)),
+            dma((3 + 2 * (heads // GROUP),)),
         ],
         compiler_params=pltpu.CompilerParams(
-            collective_id=0, has_side_effects=True, vmem_limit_bytes=60 * 1024 * 1024
+            collective_id=0, has_side_effects=True, vmem_limit_bytes=32 * 1024 * 1024
         ),
-    )(tokens[0], in_gain[None], w_query, w_key, w_value, w_out, out_gain[None], covis_list, covis_count)
+    )(*(pltpu.with_memory_space_constraint(a, pltpu.HBM) for a in (tokens[0], in_gain[None], w_query, w_key, w_value, w_out, out_gain[None], covis_list)), covis_count)
     return out[None]
 
 

time: 33.6 us -> 31.2 us (0.929)
  Pallas kernels: 31.1 us -> 29.6 us
  local copies, waits for them, and re-layouts: 1.67 us -> 0.71 us
    pallas_call x1, Pallas kernels: 31.1 us -> 29.6 us  [on_device(): pl.pallas_call(functools.partial(body, views), out_shape=jax.ShapeDtypeSt...]
    unnamed x1, local copies, waits for them, and re-layouts: 1.67 us -> 0.71 us
where the time goes in v2:
time: 31.2 us; the launch traced here: 31 us
  Pallas kernels  29.6 us (95%)
  local copies, waits for them, and re-layouts  0.71 us (2%)
  between operations  0.66 us (2%)
    pallas_call x1, Pallas kernels, on_device(): pl.pallas_call(functools.partial(body, views), out_shape=jax.ShapeDtypeSt...  29.6 us
    unnamed x1, local copies, waits for them, and re-layouts  0.71 us

profile of v2, /device:TPU:17, one launch (start us, length us, event | category | flops | bytes accessed | tf_op | source)
XLA Modules:
  0.0 31.0 jit_solution(2868358428985467842)
XLA Ops:
  0.7 29.6 %shard_map.91 = bf16[128,1024]{1,0:T(8,128)(2,1)S(1)} custom-call(bf16[128,1024]{1,0:T(8,128)(2,1)} %bitcast.5, f32[1,1024]{1,0:T(1,128)} %bitcast.6, bf16[1024,1024]{1,0:T(8,128)(2,1)} %wq_hbm.1, bf16[1024,1024]{1,0:T(8,128)(2,1)} %wk_hbm.1, bf16[1024,1024]{1,0:T(8,128)(2,1)} %wv_hbm.1, bf16[1024,1024]{1,0:T(8,128)(2,1)} %wo_hbm.1, f32[1,1024]{1,0:T(1,128)} %bitcast.7, ...), custom_call_target="tpu_custom_call" | custom-call | tf_op jit(solution)/shard_map/pallas_call | solution.py:422
  30.3 0.7 %copy.12 = bf16[1,128,1024]{2,1,0:T(8,128)(2,1)} copy(bf16[1,128,1024]{2,1,0:T(8,128)(2,1)S(1)} %bitcast.4) | data formatting | bytes 524288

commit v3 on v2

--- a/solution.py
+++ b/solution.py
@@ -62,6 +62,7 @@
     out_ref,
     buf, other, wq, wk, wv, wo, in_gain, out_gain, lists, counts, qpad, kbuf, vtbuf,
     peaks, totals, acc, mask, stats_out, stats_in, acc_in,
+    s_even, s_odd, w_even, w_odd, keeps,
     load_sem, send_sem, recv_sem, misc_send, misc_recv,
 ):
     chips = views // 2
@@ -273,56 +274,80 @@
     loads[5].wait()
     loads[6].wait()
 
-    def project(first, second, keys, values):
+    queries = 2 * rows
+    tiles = rows // 16
+
+    def project(first, second):
         normed = normed_of(jnp.concatenate([first, second], axis=0))
-        keys[...] = jnp.dot(normed, wk[...], preferred_element_type=jnp.float32).astype(jnp.bfloat16)
+        key = jnp.dot(normed, wk[...], preferred_element_type=jnp.float32).astype(jnp.bfloat16)
+        for pair in range(heads // 2):
+            kbuf[pair] = key[:, pair * 2 * HEAD_DIM:(pair + 1) * 2 * HEAD_DIM]
         value = jnp.dot(normed, wv[...], preferred_element_type=jnp.float32)
-        values[...] = value.T.astype(jnp.bfloat16)
-
-    def attend(near, far, keys, values, handed=None):
+        vtbuf[...] = value.T.astype(jnp.bfloat16).reshape(vtbuf.shape)
+
+    def score(pair, at, scores):
+        scores[at] = jnp.dot(kbuf[pair], qpad[2 * pair + at], preferred_element_type=jnp.float32)
+
+    def weigh(pair, at, scores, weights, keep_ref, on_first, on_second):
+        h = 2 * pair + at
+        found = scores[at].reshape(2 * tiles, 8, queries)
+        first, second = found[:tiles], found[tiles:]
+        old = peaks[h]
+        new = jnp.maximum(
+            jnp.where(on_first, jnp.max(first, axis=0), -INF),
+            jnp.where(on_second, jnp.max(second, axis=0), -INF),
+        )
+        new = jnp.maximum(old, jnp.broadcast_to(jnp.max(new, axis=0, keepdims=True), (8, queries)))
+        e_first = jnp.exp(first - jnp.where(on_first, new, INF)[None])
+        e_second = jnp.exp(second - jnp.where(on_second, new, INF)[None])
+        keep = jnp.exp(old - new)
+        peaks[h] = new
+        keep_ref[at] = keep
+        totals[h] = totals[h] * keep + (jnp.sum(e_first, axis=0) + jnp.sum(e_second, axis=0))
+        weights[at] = jnp.concatenate([e_first, e_second], axis=0).reshape(rows, queries).astype(jnp.bfloat16)
+
+    def gather(pair, at, weights, keep_ref):
+        h = 2 * pair + at
+        kept = acc[h].reshape(HEAD_DIM // 8, 8, queries) * keep_ref[at][None]
+        acc[h] = kept.reshape(HEAD_DIM, queries) + jnp.dot(
+            vtbuf[h], weights[at], preferred_element_type=jnp.float32
+        )
+
+    def attend(near, far, handed=None):
         on_first, on_second = mask[near] > 0.5, mask[far] > 0.5
-        span = keys.shape[0]
-        tiles = span // 16
-        queries = 2 * rows
-
-        def scores_of(h):
-            pair = (h // 2) * 2 * HEAD_DIM
-            scores = jnp.dot(keys[:, pair:pair + 2 * HEAD_DIM], qpad[h], preferred_element_type=jnp.float32)
-            return scores.reshape(2 * tiles, 8, queries)
-
-        def finish(p):
-            h, keep, weights = p
-            feats = slice(h * HEAD_DIM, (h + 1) * HEAD_DIM)
-            kept = acc[feats, :].reshape(HEAD_DIM // 8, 8, queries) * keep[None]
-            acc[feats, :] = kept.reshape(HEAD_DIM, queries) + jnp.dot(
-                values[feats, :], weights, preferred_element_type=jnp.float32
-            )
-            if handed is not None and (h + 1) % GROUP == 0:
-                handed(h // GROUP)
-
-        waiting = scores_of(0)
-        pend = None
-        for h in range(heads):
-            scores = waiting
-            if h + 1 < heads:
-                waiting = scores_of(h + 1)
-            first, second = scores[:tiles], scores[tiles:]
-            old = peaks[h]
-            new = jnp.maximum(
-                jnp.where(on_first, jnp.max(first, axis=0), -INF),
-                jnp.where(on_second, jnp.max(second, axis=0), -INF),
-            )
-            new = jnp.maximum(old, jnp.broadcast_to(jnp.max(new, axis=0, keepdims=True), (8, queries)))
-            e_first = jnp.exp(first - jnp.where(on_first, new, INF)[None])
-            e_second = jnp.exp(second - jnp.where(on_second, new, INF)[None])
-            keep = jnp.exp(old - new)
-            peaks[h] = new
-            totals[h] = totals[h] * keep + (jnp.sum(e_first, axis=0) + jnp.sum(e_second, axis=0))
-            weights = jnp.concatenate([e_first, e_second], axis=0).reshape(span, queries).astype(jnp.bfloat16)
-            if pend is not None:
-                finish(pend)
-            pend = (h, keep, weights)
-        finish(pend)
+        pairs = heads // 2
+        sides = ((s_even, w_even, keeps.at[0]), (s_odd, w_odd, keeps.at[1]))
+
+        def stage(pair, odd, ahead=True, behind=True):
+            scores, weights, keep = sides[odd]
+            next_scores, last_weights, last_keep = sides[1 - odd]
+            for at in range(2):
+                if ahead:
+                    score(pair + 1, at, next_scores)
+                if behind:
+                    gather(pair - 1, at, last_weights, last_keep)
+                weigh(pair, at, scores, weights, keep, on_first, on_second)
+
+        for at in range(2):
+            score(0, at, s_even)
+        stage(0, 0, behind=False)
+        if handed is None:
+            def both(i, carry):
+                stage(2 * i + 1, 1)
+                stage(2 * i + 2, 0)
+                return carry
+
+            lax.fori_loop(0, pairs // 2 - 1, both, 0)
+        else:
+            for pair in range(1, pairs - 1):
+                stage(pair, pair % 2)
+                if (pair * 2) % GROUP == 0:
+                    handed(pair * 2 // GROUP - 1)
+        stage(pairs - 1, 1, ahead=False)
+        for at in range(2):
+            gather(pairs - 1, at, w_odd, keeps.at[1])
+        if handed is not None:
+            handed(groups - 1)
 
     def pick(table, j):
         found = table[0]
@@ -341,9 +366,9 @@
         near, near_half, far, far_half = picks
         near_row = pl.multiple_of(near_half * half, half)
         far_row = pl.multiple_of(far_half * half, half)
-        project(buf[near, pl.ds(near_row, half)], buf[far, pl.ds(far_row, half)], kbuf, vtbuf)
+        project(buf[near, pl.ds(near_row, half)], buf[far, pl.ds(far_row, half)])
         poll(j, 0)
-        attend(near, far, kbuf, vtbuf)
+        attend(near, far)
         poll(j, 1)
         return carry
 
@@ -353,8 +378,8 @@
         return partner_copy(stats_out.at[group], stats_in.at[group], 3 + group)
 
     def acc_swap(group):
-        feats = pl.ds(group * GROUP * HEAD_DIM, GROUP * HEAD_DIM)
-        return partner_copy(acc.at[feats, pl.ds(rows, rows)], acc_in.at[feats], 3 + groups + group)
+        members = pl.ds(group * GROUP, GROUP)
+        return partner_copy(acc.at[members, :, pl.ds(rows, rows)], acc_in.at[members], 3 + groups + group)
 
     def totals_of(h, side):
         return jnp.sum(totals[h][:, side * rows:(side + 1) * rows], axis=0, keepdims=True)
@@ -372,8 +397,8 @@
     else:
         near, far = (jnp.int32(OUTER_STEPS[-1][at]) for at in (0, 2))
     span = pl.ds(half, half)
-    project(buf[near, span], buf[far, span], kbuf, vtbuf)
-    attend(near, far, kbuf, vtbuf, hand)
+    project(buf[near, span], buf[far, span])
+    attend(near, far, hand)
 
     loads[7].wait()
     loads[8].wait()
@@ -383,12 +408,11 @@
         acc_swap(group).wait_recv()
         pieces = []
         for at, h in enumerate(range(group * GROUP, (group + 1) * GROUP)):
-            feats = slice(h * HEAD_DIM, (h + 1) * HEAD_DIM)
             peak, peak_in = peaks[h][:1, :rows], stats_in[group, at:at + 1, :]
             new = jnp.maximum(peak, peak_in)
             keep, keep_in = jnp.exp(peak - new), jnp.exp(peak_in - new)
             total = totals_of(h, 0) * keep + stats_in[group, GROUP + at:GROUP + at + 1, :] * keep_in
-            attended = (acc[feats, :rows] * keep + acc_in[feats, :] * keep_in) / total
+            attended = (acc[h, :, :rows] * keep + acc_in[h] * keep_in) / total
             mean_sq = jnp.mean(attended * attended, axis=0, keepdims=True)
             pieces.append(attended * lax.rsqrt(mean_sq + 1e-6))
         feats = slice(group * GROUP * HEAD_DIM, (group + 1) * GROUP * HEAD_DIM)
@@ -436,15 +460,20 @@
             pltpu.VMEM((2, 1, slots_listed), jnp.int32),
             pltpu.VMEM((2, 1), jnp.int32),
             pltpu.VMEM((heads, 2 * HEAD_DIM, 2 * rows), bf16),
-            pltpu.VMEM((rows, width), bf16),
-            pltpu.VMEM((width, rows), bf16),
+            pltpu.VMEM((heads // 2, rows, 2 * HEAD_DIM), bf16),
+            pltpu.VMEM((heads, HEAD_DIM, rows), bf16),
             pltpu.VMEM((heads, 8, 2 * rows), f32),
             pltpu.VMEM((heads, 8, 2 * rows), f32),
-            pltpu.VMEM((width, 2 * rows), f32),
+            pltpu.VMEM((heads, HEAD_DIM, 2 * rows), f32),
             pltpu.VMEM((SLOTS, 8, 2 * rows), f32),
             pltpu.VMEM((heads // GROUP, 2 * GROUP, rows), f32),
             pltpu.VMEM((heads // GROUP, 2 * GROUP, rows), f32),
-            pltpu.VMEM((width, rows), f32),
+            pltpu.VMEM((heads, HEAD_DIM, rows), f32),
+            pltpu.VMEM((2, rows, 2 * rows), f32),
+            pltpu.VMEM((2, rows, 2 * rows), f32),
+            pltpu.VMEM((2, rows, 2 * rows), bf16),
+            pltpu.VMEM((2, rows, 2 * rows), bf16),
+            pltpu.VMEM((2, 2, 8, 2 * rows), f32),
             dma((9,)),
             dma((8, PARTS)),
             dma((SLOTS, PARTS)),

time: 31.2 us -> 29.6 us (0.949)
  the two profiles are of different devices: /device:TPU:17 before, /device:TPU:1 now
where the time goes in v3:
time: 29.6 us; the launch traced here: 29.2 us
  Pallas kernels  27.8 us (94%)
  local copies, waits for them, and re-layouts  0.71 us (2%)
  between operations  0.66 us (2%)
    pallas_call x1, Pallas kernels, on_device(): pl.pallas_call(functools.partial(body, views), out_shape=jax.ShapeDtypeSt...  27.8 us
    unnamed x1, local copies, waits for them, and re-layouts  0.71 us

profile of v3, /device:TPU:1, one launch (start us, length us, event | category | flops | bytes accessed | tf_op | source)
XLA Modules:
  0.0 29.2 jit_solution(5349135265329226155)
XLA Ops:
  0.7 27.8 %shard_map.91 = bf16[128,1024]{1,0:T(8,128)(2,1)S(1)} custom-call(bf16[128,1024]{1,0:T(8,128)(2,1)} %bitcast.5, f32[1,1024]{1,0:T(1,128)} %bitcast.6, bf16[1024,1024]{1,0:T(8,128)(2,1)} %wq_hbm.1, bf16[1024,1024]{1,0:T(8,128)(2,1)} %wk_hbm.1, bf16[1024,1024]{1,0:T(8,128)(2,1)} %wv_hbm.1, bf16[1024,1024]{1,0:T(8,128)(2,1)} %wo_hbm.1, f32[1,1024]{1,0:T(1,128)} %bitcast.7, ...), custom_call_target="tpu_custom_call" | custom-call | tf_op jit(solution)/shard_map/pallas_call | solution.py:446
  28.5 0.7 %copy.12 = bf16[1,128,1024]{2,1,0:T(8,128)(2,1)} copy(bf16[1,128,1024]{2,1,0:T(8,128)(2,1)S(1)} %bitcast.4) | data formatting | bytes 524288

commit v4 on v3

--- a/solution.py
+++ b/solution.py
@@ -213,7 +213,7 @@
             arrived(6, r - 9)
 
     inner_polls = {
-        0: ((0,), (1, 2, 3)), 1: ((4,), (5,)), 2: ((6,), (7,)), 3: ((8,), ()), 4: ((9,), (10,)), 5: ((11,), (12,)),
+        0: ((0,), (1, 2, 3)), 1: ((4,), (5,)), 2: ((6,), (7,)), 3: ((), (8,)), 4: ((9,), (10,)), 5: ((11,), (12,)),
     }
 
     def poll(j, second):
@@ -400,6 +400,15 @@
     project(buf[near, span], buf[far, span])
     attend(near, far, hand)
 
+    for part in range(PARTS):
+        for kind in range(6):
+            send(kind, None, 1, part, partner).wait_send()
+        if grid:
+            @pl.when(jnp.logical_not(outer))
+            def _(part=part):
+                send(6, None, 1, part, partner).wait_send()
+    for copy in first_copies:
+        copy.wait_send()
     loads[7].wait()
     loads[8].wait()
     update = buf[0].astype(jnp.float32)
@@ -420,15 +429,6 @@
         update = update + jnp.dot(head_normed, wo[feats, :], preferred_element_type=jnp.float32)
     out_ref[...] = update.astype(out_ref.dtype)
 
-    for part in range(PARTS):
-        for kind in range(6):
-            send(kind, None, 1, part, partner).wait_send()
-        if grid:
-            @pl.when(jnp.logical_not(outer))
-            def _(part=part):
-                send(6, None, 1, part, partner).wait_send()
-    for copy in first_copies:
-        copy.wait_send()
     for group in range(groups):
         stats_swap(group).wait_send()
         acc_swap(group).wait_send()

time: 29.6 us -> 29.3 us (0.990)
  no operation moved by 1% of the time
where the time goes in v4:
time: 29.3 us; the launch traced here: 29.1 us
  Pallas kernels  27.8 us (95%)
  local copies, waits for them, and re-layouts  0.71 us (2%)
  between operations  0.66 us (2%)
    pallas_call x1, Pallas kernels, on_device(): pl.pallas_call(functools.partial(body, views), out_shape=jax.ShapeDtypeSt...  27.8 us
    unnamed x1, local copies, waits for them, and re-layouts  0.71 us

profile of v4, /device:TPU:1, one launch (start us, length us, event | category | flops | bytes accessed | tf_op | source)
XLA Modules:
  0.0 29.1 jit_solution(2542183065889599544)
XLA Ops:
  0.7 27.8 %shard_map.91 = bf16[128,1024]{1,0:T(8,128)(2,1)S(1)} custom-call(bf16[128,1024]{1,0:T(8,128)(2,1)} %bitcast.5, f32[1,1024]{1,0:T(1,128)} %bitcast.6, bf16[1024,1024]{1,0:T(8,128)(2,1)} %wq_hbm.1, bf16[1024,1024]{1,0:T(8,128)(2,1)} %wk_hbm.1, bf16[1024,1024]{1,0:T(8,128)(2,1)} %wv_hbm.1, bf16[1024,1024]{1,0:T(8,128)(2,1)} %wo_hbm.1, f32[1,1024]{1,0:T(1,128)} %bitcast.7, ...), custom_call_target="tpu_custom_call" | custom-call | tf_op jit(solution)/shard_map/pallas_call | solution.py:446
  28.4 0.7 %copy.12 = bf16[1,128,1024]{2,1,0:T(8,128)(2,1)} copy(bf16[1,128,1024]{2,1,0:T(8,128)(2,1)S(1)} %bitcast.4) | data formatting | bytes 524288

commit v5 on v4

--- a/solution.py
+++ b/solution.py
@@ -286,10 +286,10 @@
         vtbuf[...] = value.T.astype(jnp.bfloat16).reshape(vtbuf.shape)
 
     def score(pair, at, scores):
-        scores[at] = jnp.dot(kbuf[pair], qpad[2 * pair + at], preferred_element_type=jnp.float32)
+        scores[at] = jnp.dot(kbuf[pair], qpad[2 * pair + at % 2], preferred_element_type=jnp.float32)
 
     def weigh(pair, at, scores, weights, keep_ref, on_first, on_second):
-        h = 2 * pair + at
+        h = 2 * pair + at % 2
         found = scores[at].reshape(2 * tiles, 8, queries)
         first, second = found[:tiles], found[tiles:]
         old = peaks[h]
@@ -307,7 +307,7 @@
         weights[at] = jnp.concatenate([e_first, e_second], axis=0).reshape(rows, queries).astype(jnp.bfloat16)
 
     def gather(pair, at, weights, keep_ref):
-        h = 2 * pair + at
+        h = 2 * pair + at % 2
         kept = acc[h].reshape(HEAD_DIM // 8, 8, queries) * keep_ref[at][None]
         acc[h] = kept.reshape(HEAD_DIM, queries) + jnp.dot(
             vtbuf[h], weights[at], preferred_element_type=jnp.float32
@@ -315,37 +315,39 @@
 
     def attend(near, far, handed=None):
         on_first, on_second = mask[near] > 0.5, mask[far] > 0.5
-        pairs = heads // 2
         sides = ((s_even, w_even, keeps.at[0]), (s_odd, w_odd, keeps.at[1]))
 
-        def stage(pair, odd, ahead=True, behind=True):
+        def score_all(group, scores):
+            for at in range(GROUP):
+                score((GROUP // 2) * group + at // 2, at, scores)
+
+        def gather_all(group, weights, keep):
+            for at in range(GROUP):
+                gather((GROUP // 2) * group + at // 2, at, weights, keep)
+
+        def stage(group, odd, ahead=True, behind=True):
             scores, weights, keep = sides[odd]
             next_scores, last_weights, last_keep = sides[1 - odd]
-            for at in range(2):
-                if ahead:
-                    score(pair + 1, at, next_scores)
-                if behind:
-                    gather(pair - 1, at, last_weights, last_keep)
-                weigh(pair, at, scores, weights, keep, on_first, on_second)
-
-        for at in range(2):
-            score(0, at, s_even)
+            if ahead:
+                score_all(group + 1, next_scores)
+            if behind:
+                gather_all(group - 1, last_weights, last_keep)
+            for at in range(GROUP):
+                weigh((GROUP // 2) * group + at // 2, at, scores, weights, keep, on_first, on_second)
+
+        score_all(0, s_even)
         stage(0, 0, behind=False)
         if handed is None:
-            def both(i, carry):
-                stage(2 * i + 1, 1)
-                stage(2 * i + 2, 0)
-                return carry
-
-            lax.fori_loop(0, pairs // 2 - 1, both, 0)
+            for group in range(1, groups - 1):
+                stage(group, group % 2)
         else:
-            for pair in range(1, pairs - 1):
-                stage(pair, pair % 2)
-                if (pair * 2) % GROUP == 0:
-                    handed(pair * 2 // GROUP - 1)
-        stage(pairs - 1, 1, ahead=False)
-        for at in range(2):
-            gather(pairs - 1, at, w_odd, keeps.at[1])
+            for group in range(1, groups - 1):
+                stage(group, group % 2)
+                handed(group - 1)
+        stage(groups - 1, 1, ahead=False)
+        if handed is not None:
+            handed(groups - 2)
+        gather_all(groups - 1, w_odd, keeps.at[1])
         if handed is not None:
             handed(groups - 1)
 
@@ -469,11 +471,11 @@
             pltpu.VMEM((heads // GROUP, 2 * GROUP, rows), f32),
             pltpu.VMEM((heads // GROUP, 2 * GROUP, rows), f32),
             pltpu.VMEM((heads, HEAD_DIM, rows), f32),
-            pltpu.VMEM((2, rows, 2 * rows), f32),
-            pltpu.VMEM((2, rows, 2 * rows), f32),
-            pltpu.VMEM((2, rows, 2 * rows), bf16),
-            pltpu.VMEM((2, rows, 2 * rows), bf16),
-            pltpu.VMEM((2, 2, 8, 2 * rows), f32),
+            pltpu.VMEM((GROUP, rows, 2 * rows), f32),
+            pltpu.VMEM((GROUP, rows, 2 * rows), f32),
+            pltpu.VMEM((GROUP, rows, 2 * rows), bf16),
+            pltpu.VMEM((GROUP, rows, 2 * rows), bf16),
+            pltpu.VMEM((2, GROUP, 8, 2 * rows), f32),
             dma((9,)),
             dma((8, PARTS)),
             dma((SLOTS, PARTS)),

time: 29.3 us -> 29 us (0.990)
  Pallas kernels: 27.8 us -> 27.5 us
where the time goes in v5:
time: 29 us; the launch traced here: 28.9 us
  Pallas kernels  27.5 us (95%)
  local copies, waits for them, and re-layouts  0.71 us (2%)
  between operations  0.66 us (2%)
    pallas_call x1, Pallas kernels, on_device(): pl.pallas_call(functools.partial(body, views), out_shape=jax.ShapeDtypeSt...  27.5 us
    unnamed x1, local copies, waits for them, and re-layouts  0.71 us

profile of v5, /device:TPU:1, one launch (start us, length us, event | category | flops | bytes accessed | tf_op | source)
XLA Modules:
  0.0 28.9 jit_solution(481047706529908620)
XLA Ops:
  0.7 27.5 %shard_map.91 = bf16[128,1024]{1,0:T(8,128)(2,1)S(1)} custom-call(bf16[128,1024]{1,0:T(8,128)(2,1)} %bitcast.5, f32[1,1024]{1,0:T(1,128)} %bitcast.6, bf16[1024,1024]{1,0:T(8,128)(2,1)} %wq_hbm.1, bf16[1024,1024]{1,0:T(8,128)(2,1)} %wk_hbm.1, bf16[1024,1024]{1,0:T(8,128)(2,1)} %wv_hbm.1, bf16[1024,1024]{1,0:T(8,128)(2,1)} %wo_hbm.1, f32[1,1024]{1,0:T(1,128)} %bitcast.7, ...), custom_call_target="tpu_custom_call" | custom-call | tf_op jit(solution)/shard_map/pallas_call | solution.py:448
  28.2 0.7 %copy.12 = bf16[1,128,1024]{2,1,0:T(8,128)(2,1)} copy(bf16[1,128,1024]{2,1,0:T(8,128)(2,1)S(1)} %bitcast.4) | data formatting | bytes 524288

commit v6 on v5

--- a/solution.py
+++ b/solution.py
@@ -260,17 +260,22 @@
         hits = jnp.where(((listed == ids) | (ids == query_view)) & valid, 1.0, 0.0)
         hit = jnp.max(hits, axis=1, keepdims=True)
         for slot in range(SLOTS):
-            mask[slot, :, side * rows:(side + 1) * rows] = jnp.broadcast_to(hit[slot:slot + 1], (8, rows))
+            mask[side, slot] = jnp.broadcast_to(hit[slot:slot + 1], (8, 2 * rows))
 
     loads[4].wait()
     query_in = jnp.concatenate([normed_of(buf[0]), normed_of(other[...])], axis=0)
     query = jnp.dot(query_in, wq[...], preferred_element_type=jnp.float32).astype(jnp.bfloat16)
     query = query.astype(jnp.float32) * HEAD_DIM ** (-0.5)
     query_t = query.T.astype(jnp.bfloat16)
-    zero = jnp.zeros((HEAD_DIM, 2 * rows), jnp.bfloat16)
-    for h in range(heads):
-        mine = query_t[h * HEAD_DIM:(h + 1) * HEAD_DIM, :]
-        qpad[h] = jnp.concatenate([mine, zero] if h % 2 == 0 else [zero, mine], axis=0)
+    zero = jnp.zeros((HEAD_DIM, rows), jnp.bfloat16)
+    for unit in range(heads):
+        pair, side = unit % (heads // 2), 1 - unit // (heads // 2)
+        first, second = (
+            query_t[h * HEAD_DIM:(h + 1) * HEAD_DIM, side * rows:(side + 1) * rows] for h in (2 * pair, 2 * pair + 1)
+        )
+        qpad[unit] = jnp.concatenate(
+            [jnp.concatenate([first, zero], axis=1), jnp.concatenate([zero, second], axis=1)], axis=0
+        )
     loads[5].wait()
     loads[6].wait()
 
@@ -279,17 +284,22 @@
 
     def project(first, second):
         normed = normed_of(jnp.concatenate([first, second], axis=0))
-        key = jnp.dot(normed, wk[...], preferred_element_type=jnp.float32).astype(jnp.bfloat16)
-        for pair in range(heads // 2):
-            kbuf[pair] = key[:, pair * 2 * HEAD_DIM:(pair + 1) * 2 * HEAD_DIM]
-        value = jnp.dot(normed, wv[...], preferred_element_type=jnp.float32)
-        vtbuf[...] = value.T.astype(jnp.bfloat16).reshape(vtbuf.shape)
-
-    def score(pair, at, scores):
-        scores[at] = jnp.dot(kbuf[pair], qpad[2 * pair + at % 2], preferred_element_type=jnp.float32)
-
-    def weigh(pair, at, scores, weights, keep_ref, on_first, on_second):
-        h = 2 * pair + at % 2
+        chunk = width // 2
+        for at in range(2):
+            columns = slice(at * chunk, (at + 1) * chunk)
+            value = jnp.dot(normed, wv[:, columns], preferred_element_type=jnp.float32)
+            vtbuf[at * heads // 4:(at + 1) * heads // 4] = value.T.astype(jnp.bfloat16).reshape(heads // 4, 2 * HEAD_DIM, rows)
+        for at in range(2):
+            key = jnp.dot(
+                normed, wk[:, at * chunk:(at + 1) * chunk], preferred_element_type=jnp.float32
+            ).astype(jnp.bfloat16)
+            for pair in range(heads // 4):
+                kbuf[at * heads // 4 + pair] = key[:, pair * 2 * HEAD_DIM:(pair + 1) * 2 * HEAD_DIM]
+
+    def score(unit, at, scores):
+        scores[at] = jnp.dot(kbuf[unit % (heads // 2)], qpad[unit], preferred_element_type=jnp.float32)
+
+    def weigh(h, at, scores, weights, keep_ref, on_first, on_second):
         found = scores[at].reshape(2 * tiles, 8, queries)
         first, second = found[:tiles], found[tiles:]
         old = peaks[h]
@@ -306,24 +316,23 @@
         totals[h] = totals[h] * keep + (jnp.sum(e_first, axis=0) + jnp.sum(e_second, axis=0))
         weights[at] = jnp.concatenate([e_first, e_second], axis=0).reshape(rows, queries).astype(jnp.bfloat16)
 
-    def gather(pair, at, weights, keep_ref):
-        h = 2 * pair + at % 2
-        kept = acc[h].reshape(HEAD_DIM // 8, 8, queries) * keep_ref[at][None]
-        acc[h] = kept.reshape(HEAD_DIM, queries) + jnp.dot(
-            vtbuf[h], weights[at], preferred_element_type=jnp.float32
-        )
+    def gather(unit, at, weights, keep_ref):
+        kept = acc[unit].reshape(HEAD_DIM // 8, 8, queries) * keep_ref[at][None]
+        found = jnp.dot(vtbuf[unit % (heads // 2)], weights[at], preferred_element_type=jnp.float32)
+        found = jnp.concatenate([found[:HEAD_DIM, :rows], found[HEAD_DIM:, rows:]], axis=1)
+        acc[unit] = kept.reshape(HEAD_DIM, queries) + found
 
     def attend(near, far, handed=None):
-        on_first, on_second = mask[near] > 0.5, mask[far] > 0.5
+        masks = [(mask[side, near] > 0.5, mask[side, far] > 0.5) for side in range(2)]
         sides = ((s_even, w_even, keeps.at[0]), (s_odd, w_odd, keeps.at[1]))
 
         def score_all(group, scores):
             for at in range(GROUP):
-                score((GROUP // 2) * group + at // 2, at, scores)
+                score(GROUP * group + at, at, scores)
 
         def gather_all(group, weights, keep):
             for at in range(GROUP):
-                gather((GROUP // 2) * group + at // 2, at, weights, keep)
+                gather(GROUP * group + at, at, weights, keep)
 
         def stage(group, odd, ahead=True, behind=True):
             scores, weights, keep = sides[odd]
@@ -333,7 +342,7 @@
             if behind:
                 gather_all(group - 1, last_weights, last_keep)
             for at in range(GROUP):
-                weigh((GROUP // 2) * group + at // 2, at, scores, weights, keep, on_first, on_second)
+                weigh(GROUP * group + at, at, scores, weights, keep, *masks[1 - 2 * group // groups])
 
         score_all(0, s_even)
         stage(0, 0, behind=False)
@@ -343,13 +352,10 @@
         else:
             for group in range(1, groups - 1):
                 stage(group, group % 2)
-                handed(group - 1)
+                if group <= groups // 2:
+                    handed(group - 1)
         stage(groups - 1, 1, ahead=False)
-        if handed is not None:
-            handed(groups - 2)
         gather_all(groups - 1, w_odd, keeps.at[1])
-        if handed is not None:
-            handed(groups - 1)
 
     def pick(table, j):
         found = table[0]
@@ -381,16 +387,16 @@
 
     def acc_swap(group):
         members = pl.ds(group * GROUP, GROUP)
-        return partner_copy(acc.at[members, :, pl.ds(rows, rows)], acc_in.at[members], 3 + groups + group)
-
-    def totals_of(h, side):
-        return jnp.sum(totals[h][:, side * rows:(side + 1) * rows], axis=0, keepdims=True)
+        return partner_copy(acc.at[members], acc_in.at[members], 3 + groups // 2 + group)
+
+    def total_of(unit):
+        return jnp.sum(totals[unit], axis=0, keepdims=True)
 
     def hand(group):
         acc_swap(group).start()
         members = range(group * GROUP, (group + 1) * GROUP)
         stats_out[group] = jnp.concatenate(
-            [peaks[h][:1, rows:] for h in members] + [totals_of(h, 1) for h in members], axis=0
+            [peaks[unit][:1] for unit in members] + [total_of(unit) for unit in members], axis=0
         )
         stats_swap(group).start()
 
@@ -414,24 +420,29 @@
     loads[7].wait()
     loads[8].wait()
     update = buf[0].astype(jnp.float32)
-    for group in range(groups):
+    for group in range(groups // 2):
         stats_swap(group).wait_recv()
         acc_swap(group).wait_recv()
-        pieces = []
-        for at, h in enumerate(range(group * GROUP, (group + 1) * GROUP)):
-            peak, peak_in = peaks[h][:1, :rows], stats_in[group, at:at + 1, :]
-            new = jnp.maximum(peak, peak_in)
-            keep, keep_in = jnp.exp(peak - new), jnp.exp(peak_in - new)
-            total = totals_of(h, 0) * keep + stats_in[group, GROUP + at:GROUP + at + 1, :] * keep_in
-            attended = (acc[h, :, :rows] * keep + acc_in[h] * keep_in) / total
-            mean_sq = jnp.mean(attended * attended, axis=0, keepdims=True)
-            pieces.append(attended * lax.rsqrt(mean_sq + 1e-6))
-        feats = slice(group * GROUP * HEAD_DIM, (group + 1) * GROUP * HEAD_DIM)
-        head_normed = (jnp.concatenate(pieces, axis=0).T * out_gain[:, feats]).astype(jnp.bfloat16)
-        update = update + jnp.dot(head_normed, wo[feats, :], preferred_element_type=jnp.float32)
+        for duo in range(2):
+            pieces = []
+            for at in (2 * duo, 2 * duo + 1):
+                theirs = group * GROUP + at
+                mine = heads // 2 + theirs
+                peak, peak_in = peaks[mine][:1], stats_in[group, at:at + 1, :]
+                new = jnp.maximum(peak, peak_in)
+                keep, keep_in = jnp.exp(peak - new), jnp.exp(peak_in - new)
+                total = total_of(mine) * keep + stats_in[group, GROUP + at:GROUP + at + 1, :] * keep_in
+                attended = (acc[mine] * keep + acc_in[theirs] * keep_in) / total
+                mean_sq = jnp.mean(attended * attended, axis=0, keepdims=True)
+                found = attended * lax.rsqrt(mean_sq + 1e-6)
+                pieces += [found[:, :rows], found[:, rows:]]
+            start = (group * GROUP + 2 * duo) * 2 * HEAD_DIM
+            feats = slice(start, start + 4 * HEAD_DIM)
+            head_normed = (jnp.concatenate(pieces, axis=0).T * out_gain[:, feats]).astype(jnp.bfloat16)
+            update = update + jnp.dot(head_normed, wo[feats, :], preferred_element_type=jnp.float32)
     out_ref[...] = update.astype(out_ref.dtype)
 
-    for group in range(groups):
+    for group in range(groups // 2):
         stats_swap(group).wait_send()
         acc_swap(group).wait_send()
 
@@ -463,14 +474,14 @@
             pltpu.VMEM((2, 1), jnp.int32),
             pltpu.VMEM((heads, 2 * HEAD_DIM, 2 * rows), bf16),
             pltpu.VMEM((heads // 2, rows, 2 * HEAD_DIM), bf16),
-            pltpu.VMEM((heads, HEAD_DIM, rows), bf16),
+            pltpu.VMEM((heads // 2, 2 * HEAD_DIM, rows), bf16),
             pltpu.VMEM((heads, 8, 2 * rows), f32),
             pltpu.VMEM((heads, 8, 2 * rows), f32),
             pltpu.VMEM((heads, HEAD_DIM, 2 * rows), f32),
-            pltpu.VMEM((SLOTS, 8, 2 * rows), f32),
-            pltpu.VMEM((heads // GROUP, 2 * GROUP, rows), f32),
-            pltpu.VMEM((heads // GROUP, 2 * GROUP, rows), f32),
-            pltpu.VMEM((heads, HEAD_DIM, rows), f32),
+            pltpu.VMEM((2, SLOTS, 8, 2 * rows), f32),
+            pltpu.VMEM((heads // GROUP // 2, 2 * GROUP, 2 * rows), f32),
+            pltpu.VMEM((heads // GROUP // 2, 2 * GROUP, 2 * rows), f32),
+            pltpu.VMEM((heads // 2, HEAD_DIM, 2 * rows), f32),
             pltpu.VMEM((GROUP, rows, 2 * rows), f32),
             pltpu.VMEM((GROUP, rows, 2 * rows), f32),
             pltpu.VMEM((GROUP, rows, 2 * rows), bf16),
@@ -479,8 +490,8 @@
             dma((9,)),
             dma((8, PARTS)),
             dma((SLOTS, PARTS)),
-            dma((3 + 2 * (heads // GROUP),)),
-            dma((3 + 2 * (heads // GROUP),)),
+            dma((3 + heads // GROUP,)),
+            dma((3 + heads // GROUP,)),
         ],
         compiler_params=pltpu.CompilerParams(
             collective_id=0, has_side_effects=True, vmem_limit_bytes=32 * 1024 * 1024

time: 29 us -> 28.9 us (level)
  no operation moved by 1% of the time
where the time goes in v6:
time: 28.9 us; the launch traced here: 28.8 us
  Pallas kernels  27.4 us (95%)
  local copies, waits for them, and re-layouts  0.71 us (2%)
  between operations  0.66 us (2%)
    pallas_call x1, Pallas kernels, on_device(): pl.pallas_call(functools.partial(body, views), out_shape=jax.ShapeDtypeSt...  27.4 us
    unnamed x1, local copies, waits for them, and re-layouts  0.71 us

profile of v6, /device:TPU:1, one launch (start us, length us, event | category | flops | bytes accessed | tf_op | source)
XLA Modules:
  0.0 28.8 jit_solution(4513166416838174483)
XLA Ops:
  0.7 27.4 %shard_map.91 = bf16[128,1024]{1,0:T(8,128)(2,1)S(1)} custom-call(bf16[128,1024]{1,0:T(8,128)(2,1)} %bitcast.5, f32[1,1024]{1,0:T(1,128)} %bitcast.6, bf16[1024,1024]{1,0:T(8,128)(2,1)} %wq_hbm.1, bf16[1024,1024]{1,0:T(8,128)(2,1)} %wk_hbm.1, bf16[1024,1024]{1,0:T(8,128)(2,1)} %wv_hbm.1, bf16[1024,1024]{1,0:T(8,128)(2,1)} %wo_hbm.1, f32[1,1024]{1,0:T(1,128)} %bitcast.7, ...), custom_call_target="tpu_custom_call" | custom-call | tf_op jit(solution)/shard_map/pallas_call | solution.py:459
  28.1 0.7 %copy.12 = bf16[1,128,1024]{2,1,0:T(8,128)(2,1)} copy(bf16[1,128,1024]{2,1,0:T(8,128)(2,1)S(1)} %bitcast.4) | data formatting | bytes 524288

commit v7 on v6

--- a/solution.py
+++ b/solution.py
@@ -141,8 +141,8 @@
         @pl.when(outer)
         def _():
             for part in range(PARTS):
+                send(2, None, 2, part, beside).start()
                 send(0, None, RELAY, part, skip).start()
-                send(2, None, 2, part, beside).start()
             for part in range(PARTS):
                 send(1, None, 1, part, along).start()
 
@@ -191,10 +191,10 @@
         send(5, 5, 5, part, along).start()
 
     def inner_poll(r):
+        if 1 <= r < 5:
+            far_on(r - 1)
         if r < PARTS:
             arrived(2, r)
-        if 1 <= r < 5:
-            far_on(r - 1)
         if r == 2:
             for part in range(3):
                 send(6, 2, 5, part, across).start()

time: 28.9 us -> 28.9 us (level)
  no operation moved by 1% of the time
where the time goes in v7:
time: 28.9 us; the launch traced here: 28.8 us
  Pallas kernels  27.4 us (95%)
  local copies, waits for them, and re-layouts  0.71 us (2%)
  between operations  0.66 us (2%)
    pallas_call x1, Pallas kernels, on_device(): pl.pallas_call(functools.partial(body, views), out_shape=jax.ShapeDtypeSt...  27.4 us
    unnamed x1, local copies, waits for them, and re-layouts  0.71 us

profile of v7, /device:TPU:1, one launch (start us, length us, event | category | flops | bytes accessed | tf_op | source)
XLA Modules:
  0.0 28.8 jit_solution(10080736139678539036)
XLA Ops:
  0.7 27.4 %shard_map.91 = bf16[128,1024]{1,0:T(8,128)(2,1)S(1)} custom-call(bf16[128,1024]{1,0:T(8,128)(2,1)} %bitcast.5, f32[1,1024]{1,0:T(1,128)} %bitcast.6, bf16[1024,1024]{1,0:T(8,128)(2,1)} %wq_hbm.1, bf16[1024,1024]{1,0:T(8,128)(2,1)} %wk_hbm.1, bf16[1024,1024]{1,0:T(8,128)(2,1)} %wv_hbm.1, bf16[1024,1024]{1,0:T(8,128)(2,1)} %wo_hbm.1, f32[1,1024]{1,0:T(1,128)} %bitcast.7, ...), custom_call_target="tpu_custom_call" | custom-call | tf_op jit(solution)/shard_map/pallas_call | solution.py:459
  28.0 0.7 %copy.12 = bf16[1,128,1024]{2,1,0:T(8,128)(2,1)} copy(bf16[1,128,1024]{2,1,0:T(8,128)(2,1)S(1)} %bitcast.4) | data formatting | bytes 524288
